TPU v7x, 256 devices: a whole 4x4x8 slice. The times are simulated.
256 devices in a mesh: blk: 32 (over z, y_lo, core), chan: 8 (over y_hi, x).
Axes of the slice: x: 4, y: 4 (y_hi: 2, y_lo: 2; y = y_hi * 2 + y_lo), z: 8, core: 2. Of those that a mesh axis runs over, the one named last changes fastest.
Arguments:
- spec_in: bfloat16 [256, 2, 512, 128], P('chan', None, 'blk'), may hold values from -6 to 6
- weight: bfloat16 [128, 2, 256, 256], P('blk', None, 'chan'), may hold values from -0.5 to 0.5
- pattern: int32 [128, 4, 4], P('blk'), may hold values 0 or 1
- cotangent: bfloat16 [256, 2, 512, 128], P('chan', None, 'blk'), may hold values from -6 to 6
Outputs:
- spec_out: bfloat16 [256, 2, 512, 128], P('chan', None, 'blk')
- grad_in: bfloat16 [256, 2, 512, 128], P('chan', None, 'blk')
- grad_weight: float32 [128, 2, 256, 256], P('blk', None, 'chan')
All inputs are finite; a program needn't handle non-finite values. No bound on the sum of `pattern` on one device may be relied on, other than what follows from the above.
Results may differ from a plain program's by a relative error of at most 0.001.
Values may be sent and summed in bfloat16 or wider, within the bound.
A program may use at most 128 MiB of HBM per device.

v0:
```python
import jax
import jax.numpy as jnp
from jax import lax
from jax.sharding import PartitionSpec as P


def mix_forward(x_real, x_imag, w_real, w_imag):
    form = "ism,mio->osm"
    real_part = jnp.einsum(form, x_real, w_real, preferred_element_type=jnp.float32) - jnp.einsum(
        form, x_imag, w_imag, preferred_element_type=jnp.float32
    )
    imag_part = jnp.einsum(form, x_real, w_imag, preferred_element_type=jnp.float32) + jnp.einsum(
        form, x_imag, w_real, preferred_element_type=jnp.float32
    )
    return jnp.stack([real_part, imag_part], axis=1)


def mix_input_grad(g_real, g_imag, w_real, w_imag):
    form = "osm,mio->ism"
    real_part = jnp.einsum(form, g_real, w_real, preferred_element_type=jnp.float32) + jnp.einsum(
        form, g_imag, w_imag, preferred_element_type=jnp.float32
    )
    imag_part = jnp.einsum(form, g_imag, w_real, preferred_element_type=jnp.float32) - jnp.einsum(
        form, g_real, w_imag, preferred_element_type=jnp.float32
    )
    return jnp.stack([real_part, imag_part], axis=1)


def mix_weight_grad(x_real, x_imag, g_real, g_imag):
    form = "ism,osm->mio"
    real_part = jnp.einsum(form, x_real, g_real, preferred_element_type=jnp.float32) + jnp.einsum(
        form, x_imag, g_imag, preferred_element_type=jnp.float32
    )
    imag_part = jnp.einsum(form, x_real, g_imag, preferred_element_type=jnp.float32) - jnp.einsum(
        form, x_imag, g_real, preferred_element_type=jnp.float32
    )
    return jnp.stack([real_part, imag_part], axis=1)


def local(spec_in, weight, pattern, cotangent):
    in_rows = spec_in.shape[0]
    width = weight.shape[3]
    block_size = width // pattern.shape[2]
    full_mask = jnp.repeat(
        jnp.repeat(pattern.astype(jnp.bfloat16), block_size, axis=1), block_size, axis=2
    )
    own_mask = lax.dynamic_slice_in_dim(full_mask, lax.axis_index("chan") * in_rows, in_rows, 1)
    masked = weight * own_mask[:, None]
    full_weight = lax.all_gather(masked, "blk", axis=0, tiled=True)
    x_real = spec_in[:, 0]
    x_imag = spec_in[:, 1]
    grad_full = lax.all_gather(cotangent, "chan", axis=0, tiled=True)
    w_real = full_weight[:, 0]
    w_imag = full_weight[:, 1]
    summed = lax.psum_scatter(
        mix_forward(x_real, x_imag, w_real, w_imag), "chan", scatter_dimension=0, tiled=True
    )
    spec_out = summed.astype(jnp.bfloat16)
    grad_in = mix_input_grad(grad_full[:, 0], grad_full[:, 1], w_real, w_imag).astype(jnp.bfloat16)
    gs_real = grad_full[:, 0]
    gs_imag = grad_full[:, 1]
    weight_sum = lax.psum_scatter(
        mix_weight_grad(x_real, x_imag, gs_real, gs_imag), "blk", scatter_dimension=0, tiled=True
    )
    grad_weight = weight_sum * own_mask[:, None].astype(jnp.float32)
    return (spec_out, grad_in, grad_weight)


def solution(mesh):
    in_specs = (
        P("chan", None, "blk", None),
        P("blk", None, "chan", None),
        P("blk", None, None),
        P("chan", None, "blk", None),
    )
    out_specs = (
        P("chan", None, "blk", None),
        P("chan", None, "blk", None),
        P("blk", None, "chan", None),
    )
    return jax.shard_map(local, mesh=mesh, in_specs=in_specs, out_specs=out_specs, check_vma=False)
```

profile of v0, /device:TPU:1, one launch (start us, length us, event | category | flops | bytes accessed | tf_op | source)
XLA Modules:
  0.0 498.4 jit_solution(17210475181012896570)
XLA Ops:
  7.2 0.7 all-gather.5.cloned.1.call-update
  7.9 0.7 convert_element_type.11
  9.3 1.6 copy_multiply_fusion
  10.9 1.0 fusion.27
  12.9 60.3 %all-gather.5.cloned.1.call-done = bf16[256,2,16,128]{3,2,1,0:T(8,128)(2,1)} async-done(((bf16[32,2,16,128]{3,2,1,0:T(8,128)(2,1)}), bf16[256,2,16,128]{3,2,1,0:T(8,128)(2,1)}) %all-gather.5.cloned.1.call-update) | async-done | bytes 2097168 | tf_op jit(solution)/shard_map/all_gather | solution.py:52
  73.2 2.9 fusion.26
  76.1 1.3 copy.52
  77.3 2.2 copy.53
  79.5 0.8 fusion.14
  80.3 0.8 add_bitcast_fusion
  81.1 0.8 fusion.8
  81.9 0.8 subtract_bitcast_fusion
  82.7 4.1 pad_maximum_fusion
  87.1 56.0 %all-gather.3.cloned.1.call-done = bf16[128,2,32,256]{3,2,0,1:T(8,128)(2,1)} async-done(((bf16[4,2,32,256]{3,2,0,1:T(8,128)(2,1)}), bf16[128,2,32,256]{3,2,0,1:T(8,128)(2,1)}) %all-gather.3.cloned.1.call-update) | async-done | bytes 4194320 | tf_op jit(solution)/shard_map/all_gather | solution.py:49
  143.1 2.2 fusion.2
  145.2 0.7 copy-done
  147.3 2.4 pad_maximum_fusion.1
  149.7 5.8 %copy.41 = f32[256,2,16,128]{3,2,1,0:T(8,128)} copy(f32[256,2,16,128]{0,2,3,1:T(8,128)} %pad_maximum_fusion.1) | data formatting | bytes 8388608 | tf_op jit(solution)/shard_map/stack | solution.py:15
  155.6 0.6 copy-done.3
  156.2 0.6 dynamic-slice
  157.5 2.4 fusion.1
  160.3 0.7 fusion.7
  161.0 0.5 copy.44
  161.5 2.4 fusion
  164.3 0.7 fusion.6
  165.0 0.5 copy.45
  165.5 0.7 pad_maximum_fusion.2
  166.3 230.7 %all-reduce.3.cloned.1.call-done = f32[128,2,32,256]{3,2,0,1:T(8,128)} async-done(((f32[128,2,32,256]{3,2,0,1:T(8,128)}), f32[128,2,32,256]{3,2,0,1:T(8,128)}) %all-reduce.3.cloned.1.call-update) | async-done | bytes 8388624
  397.0 1.0 dynamic-slice_multiply_fusion
  398.0 0.7 copy.46
  398.7 91.4 %reduce-scatter.5.cloned.1.call-done = f32[32,2,16,128]{3,2,1,0:T(8,128)} async-done(((f32[256,2,16,128]{3,2,1,0:T(8,128)}), f32[32,2,16,128]{3,2,1,0:T(8,128)}) %reduce-scatter.5.cloned.1.call-update) | async-done | bytes 524304 | tf_op jit(solution)/shard_map/reduce_scatter | solution.py:55
  490.1 1.8 convert_element_type.12
  (25 shorter events, 4.2 us)
Async XLA Ops:
  7.2 66.0 %all-gather.5.cloned.1.call-start = ((), (), s32[]{:S(2)}) async-start(), calls=%async_computation.3 | async-start | bytes 2359296 | tf_op jit(solution)/shard_map/all_gather | solution.py:52
  7.9 135.2 %all-gather.3.cloned.1.call-start = ((), (), s32[]{:S(2)}) async-start(), calls=%async_computation.1 | async-start | bytes 4325376 | tf_op jit(solution)/shard_map/all_gather | solution.py:49
  10.9 386.1 %all-reduce.3.cloned.1.call-start = ((), (), s32[]{:S(2)}) async-start(), calls=%async_computation.4 | async-start | bytes 16777216
  86.9 403.2 %reduce-scatter.5.cloned.1.call-start = ((), (), s32[]{:S(2)}) async-start(), calls=%async_computation.2 | async-start | bytes 4718592 | tf_op jit(solution)/shard_map/reduce_scatter | solution.py:55
  143.1 2.8 copy-start
  155.5 0.7 copy-start.3
  157.4 2.8 copy-start.1
  161.5 2.8 copy-start.2
Sparse Core Ops, SparseCore 0:
  10.6 62.5 all-gather.4
  75.6 67.3 all-gather.2
  145.7 251.2 all-reduce.2
  401.0 89.0 reduce-scatter.4
where the time goes:
time: 499 us; the launch traced here: 498 us
  waiting for transfers between devices  439 us (88%)
  local copies, waits for them, and re-layouts  19.2 us (4%)
  between operations  14.6 us (3%)
  matrix products  12.9 us (3%)
  other arithmetic  12.3 us (2%)
    unnamed x5, waiting for transfers between devices  231 us
    reduce_scatter x1, waiting for transfers between devices, local(): lax.psum_scatter(mix_forward(x_real, x_imag, w_real, w_imag), 'chan', sca...  91.4 us
    all_gather x1, waiting for transfers between devices, local(): grad_full = lax.all_gather(cotangent, 'chan', axis=0, tiled=True)  60.3 us
    all_gather x1, waiting for transfers between devices, local(): full_weight = lax.all_gather(masked, 'blk', axis=0, tiled=True)  56 us
  transfers between devices with their start and end apart: 4, of which 4 were waited for; matrix products, arithmetic and copies ran while one was open for 8% of the time, Pallas kernels for 0%

commit v1 on v0

v1 whole, which is shorter than its diff:
```python
import jax
import jax.numpy as jnp
from jax import lax
from jax.experimental import pallas as pl
from jax.experimental.pallas import tpu as pltpu
from jax.sharding import PartitionSpec as P

F32 = jnp.float32
BF16 = jnp.bfloat16
MESH = pl.DeviceIdType.MESH

NZ, NYL, NC, NYH, NX = 8, 2, 2, 2, 4
NJ = NZ * NYL
NCH = NYH * NX
NCHIP = NJ * NCH
CH = 32
S = 16
C = 256


def kernel(x_ref, w_ref, pat_ref, g_ref, out_ref, gin_ref, gw_ref,
           xf, b32, sbuf, xm, wmask, wrecv, wb, ebuf, ybuf, rbuf, gall, gwbuf, gwr,
           x_send, x_recv, x_loc, w_send, w_recv, y_send, y_recv, y_loc, d_send, d_recv):
    blk = lax.axis_index("blk")
    c = lax.axis_index("chan")
    core = blk % NC
    j = blk // NC
    z = j // NYL
    y = (c // NX) * NYL + j % NYL
    x = c % NX

    def at(t):
        tz = (z + t % NZ) % NZ
        ty = (y + (t // NZ) % (NYL * NYH)) % (NYL * NYH)
        tx = (x + t // (NZ * NYL * NYH)) % NX
        return tz * NYL + ty % NYL, (ty // NYL) * NX + tx

    barrier = pltpu.get_barrier_semaphore()

    def greet(t, carry):
        tj, tc = at(t)
        pl.semaphore_signal(barrier, inc=1, device_id={"blk": tj * NC + core, "chan": tc}, device_id_type=MESH)
        return carry

    lax.fori_loop(1, NCHIP, greet, 0)

    def greet_other(k, carry):
        pl.semaphore_signal(barrier, inc=1, device_id={"blk": j * NC + 1 - core, "chan": k}, device_id_type=MESH)
        return carry

    lax.fori_loop(0, NCH, greet_other, 0)

    lane = lax.broadcasted_iota(jnp.int32, (1, C), 1) // 64

    def mask_row(k):
        row = jnp.zeros((1, C), F32)
        for b in range(4):
            row = jnp.where(lane == b, pat_ref[k, c // 2, b].astype(F32), row)
        return row

    for k in range(4):
        row = mask_row(k)
        for p in range(2):
            wmask[k, p] = (w_ref[k, p].astype(F32) * row).astype(BF16)

    xf[0:1024, :] = x_ref[...].reshape(1024, 128).astype(F32)
    xf[1024:2048, :] = g_ref[...].reshape(1024, 128).astype(F32)
    for s in range(S):
        rows = [xf[pl.ds(q * 1024 + p * S + s, CH, stride=2 * S), :] for q in range(2) for p in range(2)]
        b32[pl.ds(s, 128, stride=S), :] = jnp.concatenate(rows, axis=0).T
    sbuf[...] = b32[...].reshape(128, S, 128).astype(BF16)

    pl.semaphore_wait(barrier, NCHIP - 1 + NCH)

    w_self = c // 4 == core
    for k in range(4):
        for other in range(NC):
            mine = (4 * core + k == c) & (core == other)

            @pl.when(mine)
            def _():
                pltpu.make_async_copy(wmask.at[k], wrecv.at[c], w_recv).start()

            @pl.when(jnp.logical_not(mine))
            def _():
                pltpu.make_async_remote_copy(
                    src_ref=wmask.at[k], dst_ref=wrecv.at[c], send_sem=w_send, recv_sem=w_recv,
                    device_id={"blk": j * NC + other, "chan": 4 * core + k}, device_id_type=MESH).start()

    def send_x(t, carry):
        tj, tc = at(t)
        pltpu.make_async_remote_copy(
            src_ref=sbuf.at[tj * NCH + tc], dst_ref=xm.at[c, pl.ds(pl.multiple_of(j * S, S), S)],
            send_sem=x_send, recv_sem=x_recv,
            device_id={"blk": tj * NC + core, "chan": tc}, device_id_type=MESH).start()
        return carry

    lax.fori_loop(1, NCHIP, send_x, 0)
    own_x = pltpu.make_async_copy(sbuf.at[j * NCH + c], xm.at[c, pl.ds(pl.multiple_of(j * S, S), S)], x_loc)
    own_x.start()

    for q in range(4):
        o = lax.broadcasted_iota(jnp.int32, (C, NCH * 128), 0)
        l = lax.broadcasted_iota(jnp.int32, (C, NCH * 128), 1)
        ebuf[q] = (l == (o // CH) * 128 + q * CH + o % CH).astype(F32).astype(BF16)

    pltpu.make_async_copy(wrecv, wrecv, w_recv).wait()
    wr = wrecv[:, 0].reshape(C, C)
    wi = wrecv[:, 1].reshape(C, C)
    wrt = wr.astype(F32).T.astype(BF16)
    wit = wi.astype(F32).T.astype(BF16)

    def spread(a, qa, b, qb):
        left = jnp.dot(a, ebuf[qa], preferred_element_type=F32)
        return (left + jnp.dot(b, ebuf[qb], preferred_element_type=F32)).astype(BF16)

    for part, rows in enumerate((spread(wr, 0, wi, 1), spread(-wi, 0, wr, 1),
                                 spread(wrt, 2, -wit, 3), spread(wit, 2, wrt, 3))):
        for k in range(NCH):
            wb[k * 128 + part * CH:k * 128 + part * CH + CH, :] = rows[k * CH:(k + 1) * CH, :]

    own_x.wait()
    pltpu.make_async_copy(sbuf.at[pl.ds(0, NCHIP - 1)], sbuf.at[pl.ds(0, NCHIP - 1)], x_recv).wait()
    full = jnp.concatenate([xm[k] for k in range(NCH)], axis=1)
    for n in range(4):
        part = jnp.dot(full, wb[:, n * 256:(n + 1) * 256], preferred_element_type=F32).astype(BF16)
        ybuf[2 * n] = part[:, :128]
        ybuf[2 * n + 1] = part[:, 128:]

    def send_y(t, carry):
        tj, tc = at(t)
        pltpu.make_async_remote_copy(
            src_ref=ybuf.at[tc, pl.ds(pl.multiple_of(tj * S, S), S)], dst_ref=rbuf.at[j * NCH + c],
            send_sem=y_send, recv_sem=y_recv,
            device_id={"blk": tj * NC + core, "chan": tc}, device_id_type=MESH).start()
        return carry

    lax.fori_loop(1, NCHIP, send_y, 0)
    own_y = pltpu.make_async_copy(ybuf.at[c, pl.ds(pl.multiple_of(j * S, S), S)], rbuf.at[j * NCH + c], y_loc)
    own_y.start()

    for h in range(2):
        gall[:, h * C:(h + 1) * C] = lax.dot_general(
            full, ebuf[2 + h], (((1,), (1,)), ((), ())), preferred_element_type=F32).astype(BF16)
    for k in range(NCH):
        both = lax.dot_general(xm[k], gall[...], (((0,), (0,)), ((), ())), preferred_element_type=F32)
        gwbuf[k, 0] = both[0:CH, :C] + both[CH:2 * CH, C:]
        gwbuf[k, 1] = both[0:CH, C:] - both[CH:2 * CH, :C]

    for k in range(NCH):
        mine = w_self & (c == k)

        @pl.when(mine)
        def _():
            pltpu.make_async_copy(gwbuf.at[k], gwr.at[core, c % 4], d_recv).start()

        @pl.when(jnp.logical_not(mine))
        def _():
            pltpu.make_async_remote_copy(
                src_ref=gwbuf.at[k], dst_ref=gwr.at[core, c % 4], send_sem=d_send, recv_sem=d_recv,
                device_id={"blk": j * NC + c // 4, "chan": k}, device_id_type=MESH).start()

    own_y.wait()
    pltpu.make_async_copy(rbuf.at[pl.ds(0, NCHIP - 1)], rbuf.at[pl.ds(0, NCHIP - 1)], y_recv).wait()
    b32[...] = rbuf[...].astype(F32).reshape(2048, 128)
    for s in range(S):
        tile = b32[pl.ds(s, 128, stride=S), :].T
        for q in range(2):
            for p in range(2):
                at_row = (2 * q + p) * CH
                xf[pl.ds(q * 1024 + p * S + s, CH, stride=2 * S), :] = tile[at_row:at_row + CH]
    out_ref[...] = xf[0:1024, :].astype(BF16).reshape(CH, 2, S, 128)
    gin_ref[...] = xf[1024:2048, :].astype(BF16).reshape(CH, 2, S, 128)

    pltpu.make_async_copy(gwr, gwr, d_recv).wait()
    for k in range(4):
        row = mask_row(k)
        for p in range(2):
            gw_ref[k, p] = (gwr[0, k, p] + gwr[1, k, p]) * row

    def sent(buf, sem):
        pltpu.make_async_copy(buf, buf, sem).wait()

    sent(sbuf.at[pl.ds(0, NCHIP - 1)], x_send)
    sent(rbuf.at[pl.ds(0, NCHIP - 1)], y_send)

    @pl.when(w_self)
    def _():
        sent(wrecv.at[pl.ds(0, NCH - 1)], w_send)
        sent(gwbuf.at[pl.ds(0, NCH - 1)], d_send)

    @pl.when(jnp.logical_not(w_self))
    def _():
        sent(wrecv, w_send)
        sent(gwbuf, d_send)


def local(spec_in, weight, pattern, cotangent):
    vmem = pl.BlockSpec(memory_space=pltpu.VMEM)
    dma = pltpu.SemaphoreType.DMA
    return pl.pallas_call(
        kernel,
        out_shape=(
            jax.ShapeDtypeStruct(spec_in.shape, BF16),
            jax.ShapeDtypeStruct(spec_in.shape, BF16),
            jax.ShapeDtypeStruct(weight.shape, F32),
        ),
        in_specs=[vmem, vmem, pl.BlockSpec(memory_space=pltpu.SMEM), vmem],
        out_specs=(vmem, vmem, vmem),
        scratch_shapes=[
            pltpu.VMEM((2048, 128), F32),
            pltpu.VMEM((2048, 128), F32),
            pltpu.VMEM((NCHIP, S, 128), BF16),
            pltpu.VMEM((NCH, NJ * S, 128), BF16),
            pltpu.VMEM((4, 2, CH, C), BF16),
            pltpu.VMEM((NCH, 2, CH, C), BF16),
            pltpu.VMEM((NCH * 128, NCH * 128), BF16),
            pltpu.VMEM((4, C, NCH * 128), BF16),
            pltpu.VMEM((NCH, NJ * S, 128), BF16),
            pltpu.VMEM((NCHIP, S, 128), BF16),
            pltpu.VMEM((NJ * S, 2 * C), BF16),
            pltpu.VMEM((NCH, 2, CH, C), F32),
            pltpu.VMEM((NC, 4, 2, CH, C), F32),
        ] + [dma] * 10,
        compiler_params=pltpu.CompilerParams(
            collective_id=0, has_side_effects=True, vmem_limit_bytes=48 << 20),
    )(spec_in, weight, pattern, cotangent)


def solution(mesh):
    in_specs = (
        P("chan", None, "blk", None),
        P("blk", None, "chan", None),
        P("blk", None, None),
        P("chan", None, "blk", None),
    )
    out_specs = (
        P("chan", None, "blk", None),
        P("chan", None, "blk", None),
        P("blk", None, "chan", None),
    )
    return jax.shard_map(local, mesh=mesh, in_specs=in_specs, out_specs=out_specs, check_vma=False)
```

time: 499 us -> 55.9 us (0.11)
  waiting for transfers between devices: 439 us -> 0 us
  Pallas kernels: 0 us -> 49.4 us
  between operations: 14.6 us -> 0.65 us
  local copies, waits for them, and re-layouts: 19.2 us -> 5.6 us
  matrix products: 12.9 us -> 0 us
  other arithmetic: 12.3 us -> 0 us
    unnamed x5 -> x0, waiting for transfers between devices: 231 us -> none
    all_gather x2 -> x0, waiting for transfers between devices: 116 us -> none  [the longest x1 60.3 us: local(): grad_full = lax.all_gather(cotangent, 'chan', axis=0, tiled=True)]
    reduce_scatter x1 -> x0, waiting for transfers between devices: 91.4 us -> none  [local(): lax.psum_scatter(mix_forward(x_real, x_imag, w_real, w_imag), 'chan', sca...]
    pallas_call x0 -> x1, Pallas kernels: none -> 49.4 us  [local(): pl.pallas_call(kernel, out_shape=(jax.ShapeDtypeStruct(spec_in.shape, BF1...]
    dot_general x12 -> x0, matrix products: 12.9 us -> none  [the longest x1 2.4 us: mix_input_grad(): jnp.einsum(form, g_real, w_real, preferred_element_type=jnp.float32)]
    another operation x3 -> x0, other arithmetic: 7.24 us -> none  [the longest x1 4.11 us: mix_weight_grad(): return jnp.stack([real_part, imag_part], axis=1)]
    another operation x3 -> x0, local copies, waits for them, and re-layouts: 6.84 us -> none  [the longest x1 5.83 us: mix_forward(): return jnp.stack([real_part, imag_part], axis=1)]
  transfers between devices with their start and end apart: 4 -> 0, of which waited for: 4 -> 0; matrix products, arithmetic and copies ran while one was open for 8% -> 0% of each run, Pallas kernels for 0% -> 0%
where the time goes in v1:
time: 55.9 us; the launch traced here: 55.7 us
  Pallas kernels  49.4 us (88%)
  local copies, waits for them, and re-layouts  5.6 us (10%)
  between operations  0.65 us (1%)
    pallas_call x1, Pallas kernels, local(): pl.pallas_call(kernel, out_shape=(jax.ShapeDtypeStruct(spec_in.shape, BF1...  49.4 us
    unnamed x11, local copies, waits for them, and re-layouts  5.6 us

profile of v1, /device:TPU:1, one launch (start us, length us, event | category | flops | bytes accessed | tf_op | source)
XLA Modules:
  0.0 55.7 jit_solution(10430114139562129344)
XLA Ops:
  0.6 0.0 copy-start
  0.6 0.9 %copy-done = bf16[32,2,16,128]{3,2,1,0:T(8,128)(2,1)S(1)} copy-done((bf16[32,2,16,128]{3,2,1,0:T(8,128)(2,1)S(1)}, bf16[32,2,16,128]{3,2,1,0:T(8,128)(2,1)}, u32[]{:S(2)}) %copy-start) | copy-done | bytes 262168
  1.6 0.0 copy-start.1
  1.6 0.9 %copy-done.1 = bf16[32,2,16,128]{3,2,1,0:T(8,128)(2,1)S(1)} copy-done((bf16[32,2,16,128]{3,2,1,0:T(8,128)(2,1)S(1)}, bf16[32,2,16,128]{3,2,1,0:T(8,128)(2,1)}, u32[]{:S(2)}) %copy-start.1) | copy-done | bytes 262168
  2.5 0.0 copy-start.2
  2.5 0.9 %copy-done.2 = bf16[4,2,32,256]{3,2,1,0:T(8,128)(2,1)S(1)} copy-done((bf16[4,2,32,256]{3,2,1,0:T(8,128)(2,1)S(1)}, bf16[4,2,32,256]{3,2,1,0:T(8,128)(2,1)}, u32[]{:S(2)}) %copy-start.2) | copy-done | bytes 131096
  3.4 0.0 copy-start.3
  3.4 0.7 %copy-done.3 = s32[4,4,4]{2,1,0:T(4,128)S(1)} copy-done((s32[4,4,4]{2,1,0:T(4,128)S(1)}, s32[4,4,4]{2,1,0:T(4,128)}, u32[]{:S(2)}) %copy-start.3) | copy-done | bytes 280
  4.1 49.4 %shard_map.67 = (bf16[32,2,16,128]{3,2,1,0:T(8,128)(2,1)S(1)}, bf16[32,2,16,128]{3,2,1,0:T(8,128)(2,1)S(1)}, f32[4,2,32,256]{3,2,1,0:T(8,128)S(1)}) custom-call(bf16[32,2,16,128]{3,2,1,0:T(8,128)(2,1)S(1)} %copy-done, bf16[4,2,32,256]{3,2,1,0:T(8,128)(2,1)S(1)} %copy-done.2, s32[4,4,4]{2,1,0:T(4,128)S(1)} %copy-done.3, bf16[32,2,16,128]{3,2,1,0:T(8,128)(2,1)S(1)} %copy-done.1), custom_call_target="tpu_custom_call" | custom-call | tf_op jit(solution)/shard_map/pallas_call | solution.py:201
  53.6 0.7 %copy.10 = bf16[32,2,16,128]{3,2,1,0:T(8,128)(2,1)} copy(bf16[32,2,16,128]{3,2,1,0:T(8,128)(2,1)S(1)} %get-tuple-element.6) | data formatting | bytes 524288
  54.3 0.7 %copy.11 = bf16[32,2,16,128]{3,2,1,0:T(8,128)(2,1)} copy(bf16[32,2,16,128]{3,2,1,0:T(8,128)(2,1)S(1)} %get-tuple-element.7) | data formatting | bytes 524288
  55.0 0.7 %copy.12 = f32[4,2,32,256]{3,2,1,0:T(8,128)} copy(f32[4,2,32,256]{3,2,1,0:T(8,128)S(1)} %get-tuple-element.8) | data formatting | bytes 524288
Async XLA Ops:
  0.6 1.0 %copy-start = (bf16[32,2,16,128]{3,2,1,0:T(8,128)(2,1)S(1)}, bf16[32,2,16,128]{3,2,1,0:T(8,128)(2,1)}, u32[]{:S(2)}) copy-start(bf16[32,2,16,128]{3,2,1,0:T(8,128)(2,1)} %x_ref.1) | copy-start | bytes 786436
  1.6 0.9 %copy-start.1 = (bf16[32,2,16,128]{3,2,1,0:T(8,128)(2,1)S(1)}, bf16[32,2,16,128]{3,2,1,0:T(8,128)(2,1)}, u32[]{:S(2)}) copy-start(bf16[32,2,16,128]{3,2,1,0:T(8,128)(2,1)} %g_ref.1) | copy-start | bytes 786436
  2.5 0.9 %copy-start.2 = (bf16[4,2,32,256]{3,2,1,0:T(8,128)(2,1)S(1)}, bf16[4,2,32,256]{3,2,1,0:T(8,128)(2,1)}, u32[]{:S(2)}) copy-start(bf16[4,2,32,256]{3,2,1,0:T(8,128)(2,1)} %w_ref.1) | copy-start | bytes 393220
  3.4 0.7 %copy-start.3 = (s32[4,4,4]{2,1,0:T(4,128)S(1)}, s32[4,4,4]{2,1,0:T(4,128)}, u32[]{:S(2)}) copy-start(s32[4,4,4]{2,1,0:T(4,128)} %pat_ref.1) | copy-start | bytes 772

commit v2 on v1

v2 whole, which is shorter than its diff:
```python
import jax
import jax.numpy as jnp
from jax import lax
from jax.experimental import pallas as pl
from jax.experimental.pallas import tpu as pltpu
from jax.sharding import PartitionSpec as P

F32 = jnp.float32
BF16 = jnp.bfloat16
MESH = pl.DeviceIdType.MESH

NZ, NYL, NC, NYH, NX = 8, 2, 2, 2, 4
NJ = NZ * NYL
NCH = NYH * NX
NCHIP = NJ * NCH
NXY = NCHIP // NZ
CH = 32
S = 16
C = 256
SLOT = NYL * S

OFFSETS = (4, 3, 5, 2, 6, 1, 7, 0)
GROUPS = ((0, 3), (3, 8))


def kernel(x_hbm, w_hbm, pat_hbm, g_hbm, rbuf, gwr, mask_ref,
           xv, gv, wv, pat_ref, xf, b32, sbuf, xm, wmask, wrecv, wb, ebuf, ybuf, gall, gwbuf,
           known, in_x, in_g, in_w, in_p, x_send, x_recv0, x_recv1, x_loc,
           w_send, w_recv, y_send, y_recv, y_loc, d_send, d_recv):
    blk = lax.axis_index("blk")
    c = lax.axis_index("chan")
    core = blk & 1
    j = blk >> 1
    z = j >> 1
    y = (c >> 2) * NYL + (j & 1)
    x = c & 3
    x_recv = (x_recv0, x_recv1)

    fetch_x = pltpu.make_async_copy(x_hbm, xv, in_x)
    fetch_g = pltpu.make_async_copy(g_hbm, gv, in_g)
    fetch_w = pltpu.make_async_copy(w_hbm, wv, in_w)
    fetch_p = pltpu.make_async_copy(pat_hbm, pat_ref, in_p)
    fetch_p.start()
    fetch_w.start()
    fetch_x.start()
    fetch_g.start()

    barrier = pltpu.get_barrier_semaphore()

    def signal(sem, b, k):
        pl.semaphore_signal(sem, inc=1, device_id={"blk": b, "chan": k}, device_id_type=MESH)

    def greet_j(t, carry):
        signal(barrier, ((j ^ t) << 1) + core, c)
        return carry

    def greet_c(t, carry):
        signal(barrier, blk, c ^ t)
        return carry

    def greet_core(t, carry):
        signal(barrier, blk ^ 1, c ^ t)
        return carry

    lax.fori_loop(1, NJ, greet_j, 0)
    lax.fori_loop(1, NCH, greet_c, 0)
    lax.fori_loop(0, NCH, greet_core, 0)

    lane = lax.broadcasted_iota(jnp.int32, (1, C), 1) // 64
    fetch_p.wait()
    fetch_w.wait()
    for k in range(4):
        row = jnp.zeros((1, C), F32)
        for b in range(4):
            row = jnp.where(lane == b, pat_ref[k, c >> 1, b].astype(F32), row)
        mask_ref[k:k + 1, :] = row
        for p in range(2):
            wmask[k, p] = (wv[k, p].astype(F32) * row).astype(BF16)

    fetch_x.wait()
    fetch_g.wait()
    xf[0:1024, :] = xv[...].reshape(1024, 128).astype(F32)
    xf[1024:2048, :] = gv[...].reshape(1024, 128).astype(F32)
    for s in range(S):
        rows = [xf[pl.ds(q * 1024 + p * S + s, CH, stride=2 * S), :] for q in range(2) for p in range(2)]
        b32[pl.ds(s, 128, stride=S), :] = jnp.concatenate(rows, axis=0).T
    sbuf[...] = b32[...].reshape(128, S, 128).astype(BF16)

    pl.semaphore_wait(barrier, NJ - 1 + NCH - 1 + NCH)

    def tell(t, carry):
        signal(known, blk, c ^ t)
        return carry

    lax.fori_loop(1, NCH, tell, 0)
    pl.semaphore_wait(known, NCH - 1)

    def xy(u):
        ty = (y + (u & 3)) & 3
        tx = (x + (u >> 2)) & 3
        return ty & 1, (ty >> 1) * NX + tx

    def rows_of(slot, yl):
        return pl.ds(pl.multiple_of(slot * SLOT + yl * S, S), S)

    own_rows = rows_of(NZ - 1, j & 1)

    def send_x(g, slot, u):
        yl, tc = xy(u)
        tj = ((z + OFFSETS[slot]) & 7) * NYL + yl
        pltpu.make_async_remote_copy(
            src_ref=sbuf.at[tj * NCH + tc], dst_ref=xm.at[c, rows_of(slot, j & 1)],
            send_sem=x_send, recv_sem=x_recv[g],
            device_id={"blk": tj * NC + core, "chan": tc}, device_id_type=MESH).start()

    def send_y(slot, u):
        yl, tc = xy(u)
        tj = ((z - OFFSETS[slot]) & 7) * NYL + yl
        pltpu.make_async_remote_copy(
            src_ref=ybuf.at[tc, rows_of(slot, yl)], dst_ref=rbuf.at[j * NCH + c],
            send_sem=y_send, recv_sem=y_recv,
            device_id={"blk": tj * NC + core, "chan": tc}, device_id_type=MESH).start()

    def send_group(g, send):
        first, last = GROUPS[g]

        def step(u, carry):
            for slot in range(first, min(last, NZ - 1)):
                send(slot, u)
            return carry

        lax.fori_loop(0, NXY, step, 0)
        if last == NZ:
            def plane(u, carry):
                send(NZ - 1, u)
                return carry

            lax.fori_loop(1, NXY, plane, 0)

    send_group(0, lambda slot, u: send_x(0, slot, u))

    w_self = (c >> 2) == core
    for k in range(4):
        for other in range(NC):
            mine = (4 * core + k == c) & (core == other)

            @pl.when(mine)
            def _():
                pltpu.make_async_copy(wmask.at[k], wrecv.at[c], w_recv).start()

            @pl.when(jnp.logical_not(mine))
            def _():
                pltpu.make_async_remote_copy(
                    src_ref=wmask.at[k], dst_ref=wrecv.at[c], send_sem=w_send, recv_sem=w_recv,
                    device_id={"blk": j * NC + other, "chan": 4 * core + k}, device_id_type=MESH).start()

    send_group(1, lambda slot, u: send_x(1, slot, u))
    own_x = pltpu.make_async_copy(sbuf.at[j * NCH + c], xm.at[c, own_rows], x_loc)
    own_x.start()

    for q in range(4):
        o = lax.broadcasted_iota(jnp.int32, (C, NCH * 128), 0)
        l = lax.broadcasted_iota(jnp.int32, (C, NCH * 128), 1)
        ebuf[q] = (l == (o // CH) * 128 + q * CH + o % CH).astype(F32).astype(BF16)

    pltpu.make_async_copy(wrecv, wrecv, w_recv).wait()
    wr = wrecv[:, 0].reshape(C, C)
    wi = wrecv[:, 1].reshape(C, C)
    wrt = wr.astype(F32).T.astype(BF16)
    wit = wi.astype(F32).T.astype(BF16)

    def spread(a, qa, b, qb):
        left = jnp.dot(a, ebuf[qa], preferred_element_type=F32)
        return (left + jnp.dot(b, ebuf[qb], preferred_element_type=F32)).astype(BF16)

    for part, rows in enumerate((spread(wr, 0, wi, 1), spread(-wi, 0, wr, 1),
                                 spread(wrt, 2, -wit, 3), spread(wit, 2, wrt, 3))):
        for k in range(NCH):
            wb[k * 128 + part * CH:k * 128 + part * CH + CH, :] = rows[k * CH:(k + 1) * CH, :]

    def load(lo, hi):
        return jnp.concatenate([xm[k, lo:hi] for k in range(NCH)], axis=1)

    def spread_grads(lo, hi):
        for h in range(2):
            gall[lo:hi, h * C:(h + 1) * C] = lax.dot_general(
                load(lo, hi), ebuf[2 + h], (((1,), (1,)), ((), ())), preferred_element_type=F32).astype(BF16)

    def products(lo, hi):
        rows = load(lo, hi)
        for n in range(4):
            part = jnp.dot(rows, wb[:, n * 256:(n + 1) * 256], preferred_element_type=F32).astype(BF16)
            ybuf[2 * n, lo:hi] = part[:, :128]
            ybuf[2 * n + 1, lo:hi] = part[:, 128:]

    cut = GROUPS[0][1] * SLOT

    def arrived(n, sem):
        pltpu.make_async_copy(sbuf.at[pl.ds(0, n)], sbuf.at[pl.ds(0, n)], sem).wait()

    arrived(GROUPS[0][1] * NXY, x_recv0)
    products(0, cut)
    send_group(0, send_y)
    spread_grads(0, cut)

    own_x.wait()
    arrived(NCHIP - 1 - GROUPS[0][1] * NXY, x_recv1)

    spread_grads(cut, NZ * SLOT)
    for k in range(NCH):
        both = lax.dot_general(xm[k], gall[...], (((0,), (0,)), ((), ())), preferred_element_type=F32)
        gwbuf[k, 0] = both[0:CH, :C] + both[CH:2 * CH, C:]
        gwbuf[k, 1] = both[0:CH, C:] - both[CH:2 * CH, :C]

    for k in range(NCH):
        mine = w_self & (c == k)

        @pl.when(mine)
        def _():
            pltpu.make_async_copy(gwbuf.at[k], gwr.at[core, c & 3], d_recv).start()

        @pl.when(jnp.logical_not(mine))
        def _():
            pltpu.make_async_remote_copy(
                src_ref=gwbuf.at[k], dst_ref=gwr.at[core, c & 3], send_sem=d_send, recv_sem=d_recv,
                device_id={"blk": j * NC + (c >> 2), "chan": k}, device_id_type=MESH).start()

    products(cut, NZ * SLOT)
    send_group(1, send_y)
    own_y = pltpu.make_async_copy(ybuf.at[c, own_rows], rbuf.at[j * NCH + c], y_loc)
    own_y.start()

    def done(buf, sem):
        pltpu.make_async_copy(buf, buf, sem).wait()

    @pl.when(w_self)
    def _():
        done(wrecv.at[pl.ds(0, NCH - 1)], w_send)
        done(gwbuf.at[pl.ds(0, NCH - 1)], d_send)

    @pl.when(jnp.logical_not(w_self))
    def _():
        done(wrecv, w_send)
        done(gwbuf, d_send)

    arrived(NCHIP - 1, x_send)
    arrived(NCHIP - 1, y_send)
    own_y.wait()
    done(gwbuf, d_recv)
    arrived(NCHIP - 1, y_recv)


def finish(rbuf, gwr, mask_ref, out_hbm, gin_hbm, gw_hbm, b32, xf, outv, ginv, gwv, s_out, s_gin, s_gw):
    for k in range(4):
        for p in range(2):
            gwv[k, p] = (gwr[0, k, p] + gwr[1, k, p]) * mask_ref[k:k + 1, :]
    put_gw = pltpu.make_async_copy(gwv, gw_hbm, s_gw)
    put_gw.start()

    b32[...] = rbuf[...].astype(F32).reshape(2048, 128)
    for s in range(S):
        tile = b32[pl.ds(s, 128, stride=S), :].T
        for q in range(2):
            for p in range(2):
                row = (2 * q + p) * CH
                xf[pl.ds(q * 1024 + p * S + s, CH, stride=2 * S), :] = tile[row:row + CH]
    outv[...] = xf[0:1024, :].astype(BF16).reshape(CH, 2, S, 128)
    put_out = pltpu.make_async_copy(outv, out_hbm, s_out)
    put_out.start()
    ginv[...] = xf[1024:2048, :].astype(BF16).reshape(CH, 2, S, 128)
    put_gin = pltpu.make_async_copy(ginv, gin_hbm, s_gin)
    put_gin.start()
    put_gw.wait()
    put_out.wait()
    put_gin.wait()


def local(spec_in, weight, pattern, cotangent):
    vmem = pl.BlockSpec(memory_space=pltpu.VMEM)
    hbm = pl.BlockSpec(memory_space=pltpu.HBM)
    dma = pltpu.SemaphoreType.DMA
    tiles, sums, mask = pl.pallas_call(
        kernel,
        out_shape=(
            jax.ShapeDtypeStruct((NCHIP, S, 128), BF16),
            jax.ShapeDtypeStruct((NC, 4, 2, CH, C), F32),
            jax.ShapeDtypeStruct((4, C), F32),
        ),
        in_specs=[hbm, hbm, hbm, hbm],
        out_specs=(vmem, vmem, vmem),
        scratch_shapes=[
            pltpu.VMEM(spec_in.shape, BF16),
            pltpu.VMEM(spec_in.shape, BF16),
            pltpu.VMEM(weight.shape, BF16),
            pltpu.SMEM(pattern.shape, jnp.int32),
            pltpu.VMEM((2048, 128), F32),
            pltpu.VMEM((2048, 128), F32),
            pltpu.VMEM((NCHIP, S, 128), BF16),
            pltpu.VMEM((NCH, NZ * SLOT, 128), BF16),
            pltpu.VMEM((4, 2, CH, C), BF16),
            pltpu.VMEM((NCH, 2, CH, C), BF16),
            pltpu.VMEM((NCH * 128, NCH * 128), BF16),
            pltpu.VMEM((4, C, NCH * 128), BF16),
            pltpu.VMEM((NCH, NZ * SLOT, 128), BF16),
            pltpu.VMEM((NZ * SLOT, 2 * C), BF16),
            pltpu.VMEM((NCH, 2, CH, C), F32),
            pltpu.SemaphoreType.REGULAR,
        ] + [dma] * 15,
        compiler_params=pltpu.CompilerParams(
            collective_id=0, has_side_effects=True, vmem_limit_bytes=40 << 20),
    )(*(pltpu.with_memory_space_constraint(a, pltpu.HBM) for a in (spec_in, weight, pattern, cotangent)))
    return pl.pallas_call(
        finish,
        out_shape=(
            jax.ShapeDtypeStruct(spec_in.shape, BF16),
            jax.ShapeDtypeStruct(spec_in.shape, BF16),
            jax.ShapeDtypeStruct(weight.shape, F32),
        ),
        in_specs=[vmem, vmem, vmem],
        out_specs=(hbm, hbm, hbm),
        scratch_shapes=[
            pltpu.VMEM((2048, 128), F32),
            pltpu.VMEM((2048, 128), F32),
            pltpu.VMEM(spec_in.shape, BF16),
            pltpu.VMEM(spec_in.shape, BF16),
            pltpu.VMEM(weight.shape, F32),
        ] + [dma] * 3,
        compiler_params=pltpu.CompilerParams(vmem_limit_bytes=16 << 20),
    )(tiles, sums, mask)


def solution(mesh):
    in_specs = (
        P("chan", None, "blk", None),
        P("blk", None, "chan", None),
        P("blk", None, None),
        P("chan", None, "blk", None),
    )
    out_specs = (
        P("chan", None, "blk", None),
        P("chan", None, "blk", None),
        P("blk", None, "chan", None),
    )
    return jax.shard_map(local, mesh=mesh, in_specs=in_specs, out_specs=out_specs, check_vma=False)
```

time: 55.9 us -> 45.1 us (0.81)
  local copies, waits for them, and re-layouts: 5.6 us -> 0 us
  Pallas kernels: 49.4 us -> 44.4 us
    unnamed x11 -> x0, local copies, waits for them, and re-layouts: 5.6 us -> none
    pallas_call x1 -> x2, Pallas kernels: 49.4 us -> 44.4 us  [the longest x1 42.6 us: local(): pl.pallas_call(kernel, out_shape=(jax.ShapeDtypeStruct((NCHIP, S, 128), B...]
where the time goes in v2:
time: 45.1 us; the launch traced here: 45 us
  Pallas kernels  44.4 us (98%)
  between operations  0.64 us (1%)
    pallas_call x1, Pallas kernels, local(): pl.pallas_call(kernel, out_shape=(jax.ShapeDtypeStruct((NCHIP, S, 128), B...  42.6 us
    pallas_call x1, Pallas kernels, local(): pl.pallas_call(finish, out_shape=(jax.ShapeDtypeStruct(spec_in.shape, BF1...  1.79 us

profile of v2, /device:TPU:1, one launch (start us, length us, event | category | flops | bytes accessed | tf_op | source)
XLA Modules:
  0.0 45.0 jit_solution(16784951660827523033)
XLA Ops:
  0.6 42.6 %shard_map.67 = (bf16[128,16,128]{2,1,0:T(8,128)(2,1)S(1)}, f32[2,4,2,32,256]{4,3,2,1,0:T(8,128)S(1)}, f32[4,256]{1,0:T(4,128)S(1)}) custom-call(bf16[32,2,16,128]{3,2,1,0:T(8,128)(2,1)} %x_hbm.1, bf16[4,2,32,256]{3,2,1,0:T(8,128)(2,1)} %w_hbm.1, s32[4,4,4]{2,1,0:T(4,128)} %pat_hbm.1, bf16[32,2,16,128]{3,2,1,0:T(8,128)(2,1)} %g_hbm.1), custom_call_target="tpu_custom_call" | custom-call | tf_op jit(solution)/shard_map/pallas_call | solution.py:282
  43.2 1.8 %shard_map.68 = (bf16[32,2,16,128]{3,2,1,0:T(8,128)(2,1)}, bf16[32,2,16,128]{3,2,1,0:T(8,128)(2,1)}, f32[4,2,32,256]{3,2,1,0:T(8,128)}) custom-call(bf16[128,16,128]{2,1,0:T(8,128)(2,1)S(1)} %get-tuple-element.6.rbuf, f32[2,4,2,32,256]{4,3,2,1,0:T(8,128)S(1)} %get-tuple-element.7.gwr, f32[4,256]{1,0:T(4,128)S(1)} %get-tuple-element.8.mask_ref), custom_call_target="tpu_custom_call" | custom-call | tf_op jit(solution)/shard_map/pallas_call | solution.py:312

commit v3 on v2

--- a/solution.py
+++ b/solution.py
@@ -24,9 +24,9 @@
 
 
 def kernel(x_hbm, w_hbm, pat_hbm, g_hbm, rbuf, gwr, mask_ref,
-           xv, gv, wv, pat_ref, xf, b32, sbuf, xm, wmask, wrecv, wb, ebuf, ybuf, gall, gwbuf,
+           xv, gv, wv, pat_ref, xf, b32, sbuf, xm, wmask, wrecv, wb, ebuf, ybuf, gall, gwbuf, gwx,
            known, in_x, in_g, in_w, in_p, x_send, x_recv0, x_recv1, x_loc,
-           w_send, w_recv, y_send, y_recv, y_loc, d_send, d_recv):
+           w_send, w_recv, h_send, h_recv, y_send, y_recv, y_loc, e_send, e_recv, d_send, d_recv):
     blk = lax.axis_index("blk")
     c = lax.axis_index("chan")
     core = blk & 1
@@ -50,21 +50,11 @@
     def signal(sem, b, k):
         pl.semaphore_signal(sem, inc=1, device_id={"blk": b, "chan": k}, device_id_type=MESH)
 
-    def greet_j(t, carry):
+    for t in range(1, NJ):
         signal(barrier, ((j ^ t) << 1) + core, c)
-        return carry
-
-    def greet_c(t, carry):
+    for t in range(1, NCH):
         signal(barrier, blk, c ^ t)
-        return carry
-
-    def greet_core(t, carry):
-        signal(barrier, blk ^ 1, c ^ t)
-        return carry
-
-    lax.fori_loop(1, NJ, greet_j, 0)
-    lax.fori_loop(1, NCH, greet_c, 0)
-    lax.fori_loop(0, NCH, greet_core, 0)
+    signal(barrier, blk ^ 1, c)
 
     lane = lax.broadcasted_iota(jnp.int32, (1, C), 1) // 64
     fetch_p.wait()
@@ -76,6 +66,24 @@
         mask_ref[k:k + 1, :] = row
         for p in range(2):
             wmask[k, p] = (wv[k, p].astype(F32) * row).astype(BF16)
+
+    pl.semaphore_wait(barrier, NJ - 1 + NCH - 1 + 1)
+    for t in range(1, NCH):
+        signal(known, blk, c ^ t)
+
+    w_self = (c >> 2) == core
+    for k in range(4):
+        mine = 4 * core + k == c
+
+        @pl.when(mine)
+        def _():
+            pltpu.make_async_copy(wmask.at[k], wrecv.at[c], w_recv).start()
+
+        @pl.when(jnp.logical_not(mine))
+        def _():
+            pltpu.make_async_remote_copy(
+                src_ref=wmask.at[k], dst_ref=wrecv.at[c], send_sem=w_send, recv_sem=w_recv,
+                device_id={"blk": blk, "chan": 4 * core + k}, device_id_type=MESH).start()
 
     fetch_x.wait()
     fetch_g.wait()
@@ -86,17 +94,8 @@
         b32[pl.ds(s, 128, stride=S), :] = jnp.concatenate(rows, axis=0).T
     sbuf[...] = b32[...].reshape(128, S, 128).astype(BF16)
 
-    pl.semaphore_wait(barrier, NJ - 1 + NCH - 1 + NCH)
-
-    def tell(t, carry):
-        signal(known, blk, c ^ t)
-        return carry
-
-    lax.fori_loop(1, NCH, tell, 0)
-    pl.semaphore_wait(known, NCH - 1)
-
     def xy(u):
-        ty = (y + (u & 3)) & 3
+        ty = y ^ (u & 3)
         tx = (x + (u >> 2)) & 3
         return ty & 1, (ty >> 1) * NX + tx
 
@@ -121,40 +120,32 @@
             send_sem=y_send, recv_sem=y_recv,
             device_id={"blk": tj * NC + core, "chan": tc}, device_id_type=MESH).start()
 
-    def send_group(g, send):
-        first, last = GROUPS[g]
-
+    def send_slots(send, first, last, start, also=None):
         def step(u, carry):
             for slot in range(first, min(last, NZ - 1)):
                 send(slot, u)
+            if also is not None:
+                also(u)
             return carry
 
-        lax.fori_loop(0, NXY, step, 0)
+        lax.fori_loop(start, NXY, step, 0)
         if last == NZ:
             def plane(u, carry):
                 send(NZ - 1, u)
                 return carry
 
-            lax.fori_loop(1, NXY, plane, 0)
-
-    send_group(0, lambda slot, u: send_x(0, slot, u))
-
-    w_self = (c >> 2) == core
-    for k in range(4):
-        for other in range(NC):
-            mine = (4 * core + k == c) & (core == other)
-
-            @pl.when(mine)
-            def _():
-                pltpu.make_async_copy(wmask.at[k], wrecv.at[c], w_recv).start()
-
-            @pl.when(jnp.logical_not(mine))
-            def _():
-                pltpu.make_async_remote_copy(
-                    src_ref=wmask.at[k], dst_ref=wrecv.at[c], send_sem=w_send, recv_sem=w_recv,
-                    device_id={"blk": j * NC + other, "chan": 4 * core + k}, device_id_type=MESH).start()
-
-    send_group(1, lambda slot, u: send_x(1, slot, u))
+            lax.fori_loop(max(start, 1), NXY, plane, 0)
+
+    def send_group(g, send, start=0):
+        send_slots(send, *GROUPS[g], start)
+
+    for u in range(2):
+        for g, (first, last) in enumerate(GROUPS):
+            for slot in range(first, last - 1 if last == NZ and u == 0 else last):
+                send_x(g, slot, u)
+    pl.semaphore_wait(known, NCH - 1)
+    send_group(0, lambda slot, u: send_x(0, slot, u), 2)
+    send_group(1, lambda slot, u: send_x(1, slot, u), 2)
     own_x = pltpu.make_async_copy(sbuf.at[j * NCH + c], xm.at[c, own_rows], x_loc)
     own_x.start()
 
@@ -163,7 +154,19 @@
         l = lax.broadcasted_iota(jnp.int32, (C, NCH * 128), 1)
         ebuf[q] = (l == (o // CH) * 128 + q * CH + o % CH).astype(F32).astype(BF16)
 
-    pltpu.make_async_copy(wrecv, wrecv, w_recv).wait()
+    hand_over = pltpu.make_async_remote_copy(
+        src_ref=wrecv, dst_ref=wrecv, send_sem=h_send, recv_sem=h_recv,
+        device_id={"blk": blk ^ 1, "chan": c}, device_id_type=MESH)
+
+    @pl.when(w_self)
+    def _():
+        pltpu.make_async_copy(wrecv, wrecv, w_recv).wait()
+        hand_over.start()
+
+    @pl.when(jnp.logical_not(w_self))
+    def _():
+        hand_over.wait_recv()
+
     wr = wrecv[:, 0].reshape(C, C)
     wi = wrecv[:, 1].reshape(C, C)
     wrt = wr.astype(F32).T.astype(BF16)
@@ -206,27 +209,41 @@
     own_x.wait()
     arrived(NCHIP - 1 - GROUPS[0][1] * NXY, x_recv1)
 
+    products(cut, NZ * SLOT)
+    send_slots(send_y, 3, 8, 0)
     spread_grads(cut, NZ * SLOT)
-    for k in range(NCH):
+    theirs, ours = 4 * (1 - core), 4 * core
+
+    def weight_grads(k):
         both = lax.dot_general(xm[k], gall[...], (((0,), (0,)), ((), ())), preferred_element_type=F32)
         gwbuf[k, 0] = both[0:CH, :C] + both[CH:2 * CH, C:]
         gwbuf[k, 1] = both[0:CH, C:] - both[CH:2 * CH, :C]
 
-    for k in range(NCH):
-        mine = w_self & (c == k)
+    for k in range(4):
+        weight_grads(theirs + k)
+    exchange = pltpu.make_async_remote_copy(
+        src_ref=gwbuf.at[pl.ds(theirs, 4)], dst_ref=gwx, send_sem=e_send, recv_sem=e_recv,
+        device_id={"blk": blk ^ 1, "chan": c}, device_id_type=MESH)
+    exchange.start()
+    for k in range(4):
+        weight_grads(ours + k)
+    exchange.wait_recv()
+    for k in range(4):
+        gwbuf[ours + k] += gwx[k]
+
+    for k in range(4):
+        mine = ours + k == c
 
         @pl.when(mine)
         def _():
-            pltpu.make_async_copy(gwbuf.at[k], gwr.at[core, c & 3], d_recv).start()
+            pltpu.make_async_copy(gwbuf.at[ours + k], gwr.at[c & 3], d_recv).start()
 
         @pl.when(jnp.logical_not(mine))
         def _():
             pltpu.make_async_remote_copy(
-                src_ref=gwbuf.at[k], dst_ref=gwr.at[core, c & 3], send_sem=d_send, recv_sem=d_recv,
-                device_id={"blk": j * NC + (c >> 2), "chan": k}, device_id_type=MESH).start()
-
-    products(cut, NZ * SLOT)
-    send_group(1, send_y)
+                src_ref=gwbuf.at[ours + k], dst_ref=gwr.at[c & 3], send_sem=d_send, recv_sem=d_recv,
+                device_id={"blk": j * NC + (c >> 2), "chan": ours + k}, device_id_type=MESH).start()
+
     own_y = pltpu.make_async_copy(ybuf.at[c, own_rows], rbuf.at[j * NCH + c], y_loc)
     own_y.start()
 
@@ -235,25 +252,27 @@
 
     @pl.when(w_self)
     def _():
-        done(wrecv.at[pl.ds(0, NCH - 1)], w_send)
-        done(gwbuf.at[pl.ds(0, NCH - 1)], d_send)
+        done(wrecv.at[pl.ds(0, 3)], w_send)
+        hand_over.wait_send()
+        done(gwr.at[pl.ds(0, 3)], d_send)
 
     @pl.when(jnp.logical_not(w_self))
     def _():
-        done(wrecv, w_send)
-        done(gwbuf, d_send)
+        done(wrecv.at[pl.ds(0, 4)], w_send)
+        done(gwr, d_send)
 
     arrived(NCHIP - 1, x_send)
     arrived(NCHIP - 1, y_send)
     own_y.wait()
-    done(gwbuf, d_recv)
+    exchange.wait_send()
+    done(gwr, d_recv)
     arrived(NCHIP - 1, y_recv)
 
 
 def finish(rbuf, gwr, mask_ref, out_hbm, gin_hbm, gw_hbm, b32, xf, outv, ginv, gwv, s_out, s_gin, s_gw):
     for k in range(4):
         for p in range(2):
-            gwv[k, p] = (gwr[0, k, p] + gwr[1, k, p]) * mask_ref[k:k + 1, :]
+            gwv[k, p] = gwr[k, p] * mask_ref[k:k + 1, :]
     put_gw = pltpu.make_async_copy(gwv, gw_hbm, s_gw)
     put_gw.start()
 
@@ -283,7 +302,7 @@
         kernel,
         out_shape=(
             jax.ShapeDtypeStruct((NCHIP, S, 128), BF16),
-            jax.ShapeDtypeStruct((NC, 4, 2, CH, C), F32),
+            jax.ShapeDtypeStruct(weight.shape, F32),
             jax.ShapeDtypeStruct((4, C), F32),
         ),
         in_specs=[hbm, hbm, hbm, hbm],
@@ -304,8 +323,9 @@
             pltpu.VMEM((NCH, NZ * SLOT, 128), BF16),
             pltpu.VMEM((NZ * SLOT, 2 * C), BF16),
             pltpu.VMEM((NCH, 2, CH, C), F32),
+            pltpu.VMEM(weight.shape, F32),
             pltpu.SemaphoreType.REGULAR,
-        ] + [dma] * 15,
+        ] + [dma] * 19,
         compiler_params=pltpu.CompilerParams(
             collective_id=0, has_side_effects=True, vmem_limit_bytes=40 << 20),
     )(*(pltpu.with_memory_space_constraint(a, pltpu.HBM) for a in (spec_in, weight, pattern, cotangent)))

time: 45.1 us -> 43.6 us (0.967)
  Pallas kernels: 44.4 us -> 42.8 us
    pallas_call x1, Pallas kernels: 42.6 us -> 41 us  [local(): pl.pallas_call(kernel, out_shape=(jax.ShapeDtypeStruct((NCHIP, S, 128), B...]
where the time goes in v3:
time: 43.6 us; the launch traced here: 43.4 us
  Pallas kernels  42.8 us (98%)
  between operations  0.64 us (1%)
    pallas_call x1, Pallas kernels, local(): pl.pallas_call(kernel, out_shape=(jax.ShapeDtypeStruct((NCHIP, S, 128), B...  41 us
    pallas_call x1, Pallas kernels, local(): pl.pallas_call(finish, out_shape=(jax.ShapeDtypeStruct(spec_in.shape, BF1...  1.78 us

profile of v3, /device:TPU:1, one launch (start us, length us, event | category | flops | bytes accessed | tf_op | source)
XLA Modules:
  0.0 43.4 jit_solution(11397020909323731158)
XLA Ops:
  0.6 41.0 %shard_map.67 = (bf16[128,16,128]{2,1,0:T(8,128)(2,1)S(1)}, f32[4,2,32,256]{3,2,1,0:T(8,128)S(1)}, f32[4,256]{1,0:T(4,128)S(1)}) custom-call(bf16[32,2,16,128]{3,2,1,0:T(8,128)(2,1)} %x_hbm.1, bf16[4,2,32,256]{3,2,1,0:T(8,128)(2,1)} %w_hbm.1, s32[4,4,4]{2,1,0:T(4,128)} %pat_hbm.1, bf16[32,2,16,128]{3,2,1,0:T(8,128)(2,1)} %g_hbm.1), custom_call_target="tpu_custom_call" | custom-call | tf_op jit(solution)/shard_map/pallas_call | solution.py:301
  41.6 1.8 %shard_map.68 = (bf16[32,2,16,128]{3,2,1,0:T(8,128)(2,1)}, bf16[32,2,16,128]{3,2,1,0:T(8,128)(2,1)}, f32[4,2,32,256]{3,2,1,0:T(8,128)}) custom-call(bf16[128,16,128]{2,1,0:T(8,128)(2,1)S(1)} %get-tuple-element.6.rbuf, f32[4,2,32,256]{3,2,1,0:T(8,128)S(1)} %get-tuple-element.7.gwr, f32[4,256]{1,0:T(4,128)S(1)} %get-tuple-element.8.mask_ref), custom_call_target="tpu_custom_call" | custom-call | tf_op jit(solution)/shard_map/pallas_call | solution.py:332

commit v4 on v3

--- a/solution.py
+++ b/solution.py
@@ -209,8 +209,6 @@
     own_x.wait()
     arrived(NCHIP - 1 - GROUPS[0][1] * NXY, x_recv1)
 
-    products(cut, NZ * SLOT)
-    send_slots(send_y, 3, 8, 0)
     spread_grads(cut, NZ * SLOT)
     theirs, ours = 4 * (1 - core), 4 * core
 
@@ -219,19 +217,21 @@
         gwbuf[k, 0] = both[0:CH, :C] + both[CH:2 * CH, C:]
         gwbuf[k, 1] = both[0:CH, C:] - both[CH:2 * CH, :C]
 
+    def exchange(k):
+        return pltpu.make_async_remote_copy(
+            src_ref=gwbuf.at[theirs + k], dst_ref=gwx.at[k], send_sem=e_send.at[k], recv_sem=e_recv.at[k],
+            device_id={"blk": blk ^ 1, "chan": c}, device_id_type=MESH)
+
     for k in range(4):
         weight_grads(theirs + k)
-    exchange = pltpu.make_async_remote_copy(
-        src_ref=gwbuf.at[pl.ds(theirs, 4)], dst_ref=gwx, send_sem=e_send, recv_sem=e_recv,
-        device_id={"blk": blk ^ 1, "chan": c}, device_id_type=MESH)
-    exchange.start()
+        exchange(k).start()
     for k in range(4):
         weight_grads(ours + k)
-    exchange.wait_recv()
-    for k in range(4):
+    products(cut, NZ * SLOT)
+    send_slots(send_y, 3, 5, 0)
+    for k in range(4):
+        exchange(k).wait_recv()
         gwbuf[ours + k] += gwx[k]
-
-    for k in range(4):
         mine = ours + k == c
 
         @pl.when(mine)
@@ -244,6 +244,7 @@
                 src_ref=gwbuf.at[ours + k], dst_ref=gwr.at[c & 3], send_sem=d_send, recv_sem=d_recv,
                 device_id={"blk": j * NC + (c >> 2), "chan": ours + k}, device_id_type=MESH).start()
 
+    send_slots(send_y, 5, 8, 0)
     own_y = pltpu.make_async_copy(ybuf.at[c, own_rows], rbuf.at[j * NCH + c], y_loc)
     own_y.start()
 
@@ -264,7 +265,8 @@
     arrived(NCHIP - 1, x_send)
     arrived(NCHIP - 1, y_send)
     own_y.wait()
-    exchange.wait_send()
+    for k in range(4):
+        exchange(k).wait_send()
     done(gwr, d_recv)
     arrived(NCHIP - 1, y_recv)
 
@@ -325,7 +327,7 @@
             pltpu.VMEM((NCH, 2, CH, C), F32),
             pltpu.VMEM(weight.shape, F32),
             pltpu.SemaphoreType.REGULAR,
-        ] + [dma] * 19,
+        ] + [dma] * 15 + [pltpu.SemaphoreType.DMA((4,))] * 2 + [dma] * 2,
         compiler_params=pltpu.CompilerParams(
             collective_id=0, has_side_effects=True, vmem_limit_bytes=40 << 20),
     )(*(pltpu.with_memory_space_constraint(a, pltpu.HBM) for a in (spec_in, weight, pattern, cotangent)))

time: 43.6 us -> 42.9 us (0.984)
  Pallas kernels: 42.8 us -> 42.2 us
    pallas_call x1, Pallas kernels: 41 us -> 40.4 us  [local(): pl.pallas_call(kernel, out_shape=(jax.ShapeDtypeStruct((NCHIP, S, 128), B...]
where the time goes in v4:
time: 42.9 us; the launch traced here: 42.8 us
  Pallas kernels  42.2 us (98%)
  between operations  0.64 us (1%)
    pallas_call x1, Pallas kernels, local(): pl.pallas_call(kernel, out_shape=(jax.ShapeDtypeStruct((NCHIP, S, 128), B...  40.4 us
    pallas_call x1, Pallas kernels, local(): pl.pallas_call(finish, out_shape=(jax.ShapeDtypeStruct(spec_in.shape, BF1...  1.78 us

profile of v4, /device:TPU:1, one launch (start us, length us, event | category | flops | bytes accessed | tf_op | source)
XLA Modules:
  0.0 42.8 jit_solution(4398451935272297584)
XLA Ops:
  0.6 40.4 %shard_map.67 = (bf16[128,16,128]{2,1,0:T(8,128)(2,1)S(1)}, f32[4,2,32,256]{3,2,1,0:T(8,128)S(1)}, f32[4,256]{1,0:T(4,128)S(1)}) custom-call(bf16[32,2,16,128]{3,2,1,0:T(8,128)(2,1)} %x_hbm.1, bf16[4,2,32,256]{3,2,1,0:T(8,128)(2,1)} %w_hbm.1, s32[4,4,4]{2,1,0:T(4,128)} %pat_hbm.1, bf16[32,2,16,128]{3,2,1,0:T(8,128)(2,1)} %g_hbm.1), custom_call_target="tpu_custom_call" | custom-call | tf_op jit(solution)/shard_map/pallas_call | solution.py:303
  41.0 1.8 %shard_map.68 = (bf16[32,2,16,128]{3,2,1,0:T(8,128)(2,1)}, bf16[32,2,16,128]{3,2,1,0:T(8,128)(2,1)}, f32[4,2,32,256]{3,2,1,0:T(8,128)}) custom-call(bf16[128,16,128]{2,1,0:T(8,128)(2,1)S(1)} %get-tuple-element.6.rbuf, f32[4,2,32,256]{3,2,1,0:T(8,128)S(1)} %get-tuple-element.7.gwr, f32[4,256]{1,0:T(4,128)S(1)} %get-tuple-element.8.mask_ref), custom_call_target="tpu_custom_call" | custom-call | tf_op jit(solution)/shard_map/pallas_call | solution.py:334

commit v5 on v4

--- a/solution.py
+++ b/solution.py
@@ -17,6 +17,7 @@
 CH = 32
 S = 16
 C = 256
+PAD_M, PAD_O = 17, 33
 SLOT = NYL * S
 
 OFFSETS = (4, 3, 5, 2, 6, 1, 7, 0)
@@ -87,12 +88,15 @@
 
     fetch_x.wait()
     fetch_g.wait()
-    xf[0:1024, :] = xv[...].reshape(1024, 128).astype(F32)
-    xf[1024:2048, :] = gv[...].reshape(1024, 128).astype(F32)
+    for q, buf in enumerate((xv, gv)):
+        for i in range(CH):
+            row = (q * CH + i) * PAD_O
+            xf[row:row + 2 * S, :] = buf[i].reshape(2 * S, 128).astype(F32)
     for s in range(S):
-        rows = [xf[pl.ds(q * 1024 + p * S + s, CH, stride=2 * S), :] for q in range(2) for p in range(2)]
-        b32[pl.ds(s, 128, stride=S), :] = jnp.concatenate(rows, axis=0).T
-    sbuf[...] = b32[...].reshape(128, S, 128).astype(BF16)
+        rows = [xf[pl.ds(q * CH * PAD_O + p * S + s, CH, stride=PAD_O), :] for q in range(2) for p in range(2)]
+        b32[pl.ds(s, NCHIP, stride=PAD_M), :] = jnp.concatenate(rows, axis=0).T
+    for m in range(NCHIP):
+        sbuf[m] = b32[m * PAD_M:m * PAD_M + S, :].astype(BF16)
 
     def xy(u):
         ty = y ^ (u & 3)
@@ -278,17 +282,21 @@
     put_gw = pltpu.make_async_copy(gwv, gw_hbm, s_gw)
     put_gw.start()
 
-    b32[...] = rbuf[...].astype(F32).reshape(2048, 128)
+    for m in range(NCHIP):
+        b32[m * PAD_M:m * PAD_M + S, :] = rbuf[m].astype(F32)
     for s in range(S):
-        tile = b32[pl.ds(s, 128, stride=S), :].T
+        tile = b32[pl.ds(s, NCHIP, stride=PAD_M), :].T
         for q in range(2):
             for p in range(2):
                 row = (2 * q + p) * CH
-                xf[pl.ds(q * 1024 + p * S + s, CH, stride=2 * S), :] = tile[row:row + CH]
-    outv[...] = xf[0:1024, :].astype(BF16).reshape(CH, 2, S, 128)
-    put_out = pltpu.make_async_copy(outv, out_hbm, s_out)
-    put_out.start()
-    ginv[...] = xf[1024:2048, :].astype(BF16).reshape(CH, 2, S, 128)
+                xf[pl.ds(q * CH * PAD_O + p * S + s, CH, stride=PAD_O), :] = tile[row:row + CH]
+    for q, buf in enumerate((outv, ginv)):
+        for o in range(CH):
+            row = (q * CH + o) * PAD_O
+            buf[o] = xf[row:row + 2 * S, :].astype(BF16).reshape(2, S, 128)
+        if q == 0:
+            put_out = pltpu.make_async_copy(outv, out_hbm, s_out)
+            put_out.start()
     put_gin = pltpu.make_async_copy(ginv, gin_hbm, s_gin)
     put_gin.start()
     put_gw.wait()
@@ -314,8 +322,8 @@
             pltpu.VMEM(spec_in.shape, BF16),
             pltpu.VMEM(weight.shape, BF16),
             pltpu.SMEM(pattern.shape, jnp.int32),
-            pltpu.VMEM((2048, 128), F32),
-            pltpu.VMEM((2048, 128), F32),
+            pltpu.VMEM((2 * CH * PAD_O, 128), F32),
+            pltpu.VMEM((NCHIP * PAD_M, 128), F32),
             pltpu.VMEM((NCHIP, S, 128), BF16),
             pltpu.VMEM((NCH, NZ * SLOT, 128), BF16),
             pltpu.VMEM((4, 2, CH, C), BF16),
@@ -341,8 +349,8 @@
         in_specs=[vmem, vmem, vmem],
         out_specs=(hbm, hbm, hbm),
         scratch_shapes=[
-            pltpu.VMEM((2048, 128), F32),
-            pltpu.VMEM((2048, 128), F32),
+            pltpu.VMEM((NCHIP * PAD_M, 128), F32),
+            pltpu.VMEM((2 * CH * PAD_O, 128), F32),
             pltpu.VMEM(spec_in.shape, BF16),
             pltpu.VMEM(spec_in.shape, BF16),
             pltpu.VMEM(weight.shape, F32),

time: 42.9 us -> 43.2 us (level)
    pallas_call x1, Pallas kernels: 1.78 us -> 1.13 us  [local(): pl.pallas_call(finish, out_shape=(jax.ShapeDtypeStruct(spec_in.shape, BF1...]
    pallas_call x1, Pallas kernels: 40.4 us -> 41 us  [local(): pl.pallas_call(kernel, out_shape=(jax.ShapeDtypeStruct((NCHIP, S, 128), B...]
where the time goes in v5:
time: 43.2 us; the launch traced here: 42.8 us
  Pallas kernels  42.2 us (98%)
  between operations  0.64 us (1%)
    pallas_call x1, Pallas kernels, local(): pl.pallas_call(kernel, out_shape=(jax.ShapeDtypeStruct((NCHIP, S, 128), B...  41 us
    pallas_call x1, Pallas kernels, local(): pl.pallas_call(finish, out_shape=(jax.ShapeDtypeStruct(spec_in.shape, BF1...  1.13 us

profile of v5, /device:TPU:1, one launch (start us, length us, event | category | flops | bytes accessed | tf_op | source)
XLA Modules:
  0.0 42.8 jit_solution(2779736689529841591)
XLA Ops:
  0.6 41.0 %shard_map.67 = (bf16[128,16,128]{2,1,0:T(8,128)(2,1)S(1)}, f32[4,2,32,256]{3,2,1,0:T(8,128)S(1)}, f32[4,256]{1,0:T(4,128)S(1)}) custom-call(bf16[32,2,16,128]{3,2,1,0:T(8,128)(2,1)} %x_hbm.1, bf16[4,2,32,256]{3,2,1,0:T(8,128)(2,1)} %w_hbm.1, s32[4,4,4]{2,1,0:T(4,128)} %pat_hbm.1, bf16[32,2,16,128]{3,2,1,0:T(8,128)(2,1)} %g_hbm.1), custom_call_target="tpu_custom_call" | custom-call | tf_op jit(solution)/shard_map/pallas_call | solution.py:311
  41.7 1.1 %shard_map.68 = (bf16[32,2,16,128]{3,2,1,0:T(8,128)(2,1)}, bf16[32,2,16,128]{3,2,1,0:T(8,128)(2,1)}, f32[4,2,32,256]{3,2,1,0:T(8,128)}) custom-call(bf16[128,16,128]{2,1,0:T(8,128)(2,1)S(1)} %get-tuple-element.6.rbuf, f32[4,2,32,256]{3,2,1,0:T(8,128)S(1)} %get-tuple-element.7.gwr, f32[4,256]{1,0:T(4,128)S(1)} %get-tuple-element.8.mask_ref), custom_call_target="tpu_custom_call" | custom-call | tf_op jit(solution)/shard_map/pallas_call | solution.py:342

commit v6 on v5

--- a/solution.py
+++ b/solution.py
@@ -88,15 +88,12 @@
 
     fetch_x.wait()
     fetch_g.wait()
-    for q, buf in enumerate((xv, gv)):
-        for i in range(CH):
-            row = (q * CH + i) * PAD_O
-            xf[row:row + 2 * S, :] = buf[i].reshape(2 * S, 128).astype(F32)
+    xf[0:1024, :] = xv[...].reshape(1024, 128).astype(F32)
+    xf[1024:2048, :] = gv[...].reshape(1024, 128).astype(F32)
     for s in range(S):
-        rows = [xf[pl.ds(q * CH * PAD_O + p * S + s, CH, stride=PAD_O), :] for q in range(2) for p in range(2)]
-        b32[pl.ds(s, NCHIP, stride=PAD_M), :] = jnp.concatenate(rows, axis=0).T
-    for m in range(NCHIP):
-        sbuf[m] = b32[m * PAD_M:m * PAD_M + S, :].astype(BF16)
+        rows = [xf[pl.ds(q * 1024 + p * S + s, CH, stride=2 * S), :] for q in range(2) for p in range(2)]
+        b32[pl.ds(s, 128, stride=S), :] = jnp.concatenate(rows, axis=0).T
+    sbuf[...] = b32[...].reshape(128, S, 128).astype(BF16)
 
     def xy(u):
         ty = y ^ (u & 3)
@@ -322,8 +319,8 @@
             pltpu.VMEM(spec_in.shape, BF16),
             pltpu.VMEM(weight.shape, BF16),
             pltpu.SMEM(pattern.shape, jnp.int32),
-            pltpu.VMEM((2 * CH * PAD_O, 128), F32),
-            pltpu.VMEM((NCHIP * PAD_M, 128), F32),
+            pltpu.VMEM((2048, 128), F32),
+            pltpu.VMEM((2048, 128), F32),
             pltpu.VMEM((NCHIP, S, 128), BF16),
             pltpu.VMEM((NCH, NZ * SLOT, 128), BF16),
             pltpu.VMEM((4, 2, CH, C), BF16),

time: 43.2 us -> 42.3 us (0.979)
  Pallas kernels: 42.2 us -> 41.5 us
    pallas_call x1, Pallas kernels: 41 us -> 40.4 us  [local(): pl.pallas_call(kernel, out_shape=(jax.ShapeDtypeStruct((NCHIP, S, 128), B...]
where the time goes in v6:
time: 42.3 us; the launch traced here: 42.2 us
  Pallas kernels  41.5 us (98%)
  between operations  0.64 us (2%)
    pallas_call x1, Pallas kernels, local(): pl.pallas_call(kernel, out_shape=(jax.ShapeDtypeStruct((NCHIP, S, 128), B...  40.4 us
    pallas_call x1, Pallas kernels, local(): pl.pallas_call(finish, out_shape=(jax.ShapeDtypeStruct(spec_in.shape, BF1...  1.13 us

profile of v6, /device:TPU:1, one launch (start us, length us, event | category | flops | bytes accessed | tf_op | source)
XLA Modules:
  0.0 42.2 jit_solution(612059107625002368)
XLA Ops:
  0.6 40.4 %shard_map.67 = (bf16[128,16,128]{2,1,0:T(8,128)(2,1)S(1)}, f32[4,2,32,256]{3,2,1,0:T(8,128)S(1)}, f32[4,256]{1,0:T(4,128)S(1)}) custom-call(bf16[32,2,16,128]{3,2,1,0:T(8,128)(2,1)} %x_hbm.1, bf16[4,2,32,256]{3,2,1,0:T(8,128)(2,1)} %w_hbm.1, s32[4,4,4]{2,1,0:T(4,128)} %pat_hbm.1, bf16[32,2,16,128]{3,2,1,0:T(8,128)(2,1)} %g_hbm.1), custom_call_target="tpu_custom_call" | custom-call | tf_op jit(solution)/shard_map/pallas_call | solution.py:308
  41.0 1.1 %shard_map.68 = (bf16[32,2,16,128]{3,2,1,0:T(8,128)(2,1)}, bf16[32,2,16,128]{3,2,1,0:T(8,128)(2,1)}, f32[4,2,32,256]{3,2,1,0:T(8,128)}) custom-call(bf16[128,16,128]{2,1,0:T(8,128)(2,1)S(1)} %get-tuple-element.6.rbuf, f32[4,2,32,256]{3,2,1,0:T(8,128)S(1)} %get-tuple-element.7.gwr, f32[4,256]{1,0:T(4,128)S(1)} %get-tuple-element.8.mask_ref), custom_call_target="tpu_custom_call" | custom-call | tf_op jit(solution)/shard_map/pallas_call | solution.py:339

commit v7 on v6

--- a/solution.py
+++ b/solution.py
@@ -21,6 +21,7 @@
 SLOT = NYL * S
 
 OFFSETS = (4, 3, 5, 2, 6, 1, 7, 0)
+TURNS = (0, 4, 8, 12, 2, 6, 10, 0)
 GROUPS = ((0, 3), (3, 8))
 
 
@@ -121,10 +122,14 @@
             send_sem=y_send, recv_sem=y_recv,
             device_id={"blk": tj * NC + core, "chan": tc}, device_id_type=MESH).start()
 
+    def turned(u, by, start):
+        v = u - start + by
+        return start + jnp.where(v >= NXY - start, v - (NXY - start), v)
+
     def send_slots(send, first, last, start, also=None):
         def step(u, carry):
             for slot in range(first, min(last, NZ - 1)):
-                send(slot, u)
+                send(slot, turned(u, TURNS[slot], start))
             if also is not None:
                 also(u)
             return carry

time: 42.3 us -> 42.7 us (level)
  Pallas kernels: 41.5 us -> 42 us
    pallas_call x1, Pallas kernels: 40.4 us -> 40.9 us  [local(): pl.pallas_call(kernel, out_shape=(jax.ShapeDtypeStruct((NCHIP, S, 128), B...]
where the time goes in v7:
time: 42.7 us; the launch traced here: 42.6 us
  Pallas kernels  42 us (98%)
  between operations  0.64 us (1%)
    pallas_call x1, Pallas kernels, local(): pl.pallas_call(kernel, out_shape=(jax.ShapeDtypeStruct((NCHIP, S, 128), B...  40.9 us
    pallas_call x1, Pallas kernels, local(): pl.pallas_call(finish, out_shape=(jax.ShapeDtypeStruct(spec_in.shape, BF1...  1.13 us

profile of v7, /device:TPU:1, one launch (start us, length us, event | category | flops | bytes accessed | tf_op | source)
XLA Modules:
  0.0 42.6 jit_solution(8621686994385746674)
XLA Ops:
  0.6 40.9 %shard_map.67 = (bf16[128,16,128]{2,1,0:T(8,128)(2,1)S(1)}, f32[4,2,32,256]{3,2,1,0:T(8,128)S(1)}, f32[4,256]{1,0:T(4,128)S(1)}) custom-call(bf16[32,2,16,128]{3,2,1,0:T(8,128)(2,1)} %x_hbm.1, bf16[4,2,32,256]{3,2,1,0:T(8,128)(2,1)} %w_hbm.1, s32[4,4,4]{2,1,0:T(4,128)} %pat_hbm.1, bf16[32,2,16,128]{3,2,1,0:T(8,128)(2,1)} %g_hbm.1), custom_call_target="tpu_custom_call" | custom-call | tf_op jit(solution)/shard_map/pallas_call | solution.py:313
  41.5 1.1 %shard_map.68 = (bf16[32,2,16,128]{3,2,1,0:T(8,128)(2,1)}, bf16[32,2,16,128]{3,2,1,0:T(8,128)(2,1)}, f32[4,2,32,256]{3,2,1,0:T(8,128)}) custom-call(bf16[128,16,128]{2,1,0:T(8,128)(2,1)S(1)} %get-tuple-element.6.rbuf, f32[4,2,32,256]{3,2,1,0:T(8,128)S(1)} %get-tuple-element.7.gwr, f32[4,256]{1,0:T(4,128)S(1)} %get-tuple-element.8.mask_ref), custom_call_target="tpu_custom_call" | custom-call | tf_op jit(solution)/shard_map/pallas_call | solution.py:344
